TPU v7x, 256 devices: a whole 4x4x8 slice. The times are simulated.
256 devices in a mesh: gx: 4 (over x), gy: 8 (over y, core), gz: 8 (over z).
Axes of the slice: x: 4, y: 4, z: 8, core: 2. Of those that a mesh axis runs over, the one named last changes fastest.
Arguments:
- fields: float32 [3, 64, 128, 1024], P(None, 'gx', 'gy', 'gz'), may hold values from -6 to 6
- diffusivity: float32 [64, 128, 1024], P('gx', 'gy', 'gz'), may hold values from 0.03 to 0.15
- velocity: float32 [3, 64, 128, 1024], P(None, 'gx', 'gy', 'gz'), may hold values from -2.4 to 2.4
- stored_snapshots: bfloat16 [127, 786432], P(None, ('gx', 'gy', 'gz')), may hold values from -36 to 36
- sample_index: int32 [262144], P(('gx', 'gy', 'gz')), may hold values from 0 to 32767, as said below
Outputs:
- new_fields: float32 [3, 64, 128, 1024], P(None, 'gx', 'gy', 'gz')
- snapshot_r: float32 [128, 128], replicated
Inputs may be any that keep to these rules, and one draw needn't show every extreme that they name: `sample_index`: entry k of a tile's list lies between k * 32 and (k + 1) * 32 - 1.
All inputs are finite; a program needn't handle non-finite values.
Results may differ from a plain program's by a relative error of at most 0.0003.
Values sent between devices are 32-bit elements; how exact they have to be, the bound alone decides.
A program may use at most 64 MiB of HBM per device.

v0:
```python
import jax
import jax.numpy as jnp
from jax import lax
from jax.sharding import PartitionSpec as P


def with_halo(array, sides, width):
    for axis, dim in sides:
        devices, length = (lax.axis_size(axis), array.shape[dim])
        up = [(i, (i + 1) % devices) for i in range(devices - 1)]
        down = [(j, i) for i, j in up]
        last = lax.slice_in_dim(array, length - width, length, axis=dim)
        first = lax.slice_in_dim(array, 0, width, axis=dim)
        before = lax.ppermute(last, axis, up)
        after = lax.ppermute(first, axis, down)
        array = jnp.concatenate([before, array, after], axis=dim)
    return array


def face_term(center_u, center_k, plus_u, plus_k, plus_v, minus_u, minus_k, minus_v):
    return (
        0.5 * (plus_k + center_k) * (plus_u - center_u)
        - 0.5 * (center_k + minus_k) * (center_u - minus_u)
        - 0.5 * (plus_v * plus_u - minus_v * minus_u)
    )


def upper_factor(gram):
    return jnp.linalg.cholesky(gram).T


def inner_rows(left, right):
    return lax.dot_general(
        left, right, (((1,), (1,)), ((), ())), preferred_element_type=jnp.float32
    )


def per_device(fields, diffusivity, velocity, stored_snapshots, sample_index):
    total_rows = (
        stored_snapshots.shape[1] * lax.axis_size("gx") * lax.axis_size("gy") * lax.axis_size("gz")
    )
    stacked = jnp.concatenate([fields, velocity, diffusivity[None]], 0)
    padded = with_halo(stacked, (("gx", 1), ("gy", 2), ("gz", 3)), 1)
    padded_u = padded[0:3]
    padded_v = padded[3:6]
    padded_k = padded[6]
    inner = (slice(1, -1), slice(1, -1), slice(1, -1))
    terms = []
    for dim in range(3):
        upper = list(inner)
        lower = list(inner)
        upper[dim] = slice(2, None)
        lower[dim] = slice(None, -2)
        upper = tuple(upper)
        lower = tuple(lower)
        terms.append(
            face_term(
                fields,
                diffusivity,
                padded_u[(slice(None),) + upper],
                padded_k[upper],
                padded_v[dim][upper],
                padded_u[(slice(None),) + lower],
                padded_k[lower],
                padded_v[dim][lower],
            )
        )
    new_fields = fields + (terms[0] + terms[1] + terms[2])
    flat_cells = new_fields.reshape(3, -1)
    sampled = jnp.take(flat_cells, sample_index, axis=1)
    new_column = sampled.reshape(1, -1).astype(jnp.bfloat16)
    snapshot_block = jnp.concatenate([stored_snapshots, new_column], 0)
    local_gram = inner_rows(snapshot_block, snapshot_block) / float(total_rows)
    whole_gram = lax.psum(local_gram, ("gx", "gy", "gz"))
    snapshot_r = upper_factor(whole_gram)
    return (new_fields, snapshot_r)


def solution(mesh):
    placed = (
        P(None, "gx", "gy", "gz"),
        P("gx", "gy", "gz"),
        P(None, "gx", "gy", "gz"),
        P(None, ("gx", "gy", "gz")),
        P(("gx", "gy", "gz")),
    )
    return jax.shard_map(
        per_device,
        mesh=mesh,
        in_specs=placed,
        out_specs=(P(None, "gx", "gy", "gz"), P()),
        check_vma=False,
    )
```

profile of v0, /device:TPU:1, one launch (start us, length us, event | category | flops | bytes accessed | tf_op | source)
XLA Modules:
  0.0 335.2 jit_solution(9069121309860138379)
XLA Ops:
  7.2 0.0 copy-start.3
  7.2 0.0 copy-start
  7.2 0.0 copy-start.1
  7.2 0.0 copy-start.11
  7.2 0.0 all-reduce.2.cloned.1.call-start
  7.3 0.9 pad_maximum_fusion.25
  8.2 3.9 %collective-permute-start = (f32[7,1,16,128]{3,2,1,0:T(8,128)S(1)}, f32[7,1,16,128]{3,2,1,0:T(8,128)S(1)}, u32[]{:S(2)}, u32[]{:S(2)}) collective-permute-start(f32[7,1,16,128]{3,2,1,0:T(8,128)S(1)} %get-tuple-element.18), channel_id=1, source_target_pairs={{0,64},{64,128},{128,192},{1,65},{65,129},{129,193},{2,66},{66,130... | collective-permute-start | bytes 172040 | tf_op jit(solution)/shard_map/ppermute | solution.py:14
  12.1 1.3 collective-permute-start.1
  13.4 0.0 collective-permute-done
  13.4 3.6 %collective-permute-done.1 = f32[7,1,16,128]{3,2,1,0:T(8,128)S(1)} collective-permute-done((f32[7,1,16,128]{3,2,1,0:T(8,128)S(1)}, f32[7,1,16,128]{3,2,1,0:T(8,128)S(1)}, u32[]{:S(2)}, u32[]{:S(2)}) %collective-permute-start.1) | collective-permute-done | bytes 57376 | tf_op jit(solution)/shard_map/ppermute | solution.py:15
  17.0 0.0 copy-start.5
  17.0 1.4 pad_maximum_fusion.22
  18.4 5.2 %collective-permute-start.2 = (f32[7,18,1,128]{3,2,1,0:T(1,128)S(1)}, f32[7,18,1,128]{3,2,1,0:T(1,128)S(1)}, u32[]{:S(2)}, u32[]{:S(2)}) collective-permute-start(f32[7,18,1,128]{3,2,1,0:T(1,128)S(1)} %get-tuple-element.16), channel_id=1, source_target_pairs={{0,8},{8,16},{16,24},{24,32},{32,40},{40,48},{48,56},{1,9},{9,17},... | collective-permute-start | bytes 193544 | tf_op jit(solution)/shard_map/ppermute | solution.py:14
  23.6 1.9 collective-permute-start.3
  25.6 0.0 copy-done.11
  25.6 0.0 collective-permute-done.2
  25.6 0.0 copy-start.7
  25.6 3.6 %collective-permute-done.3 = f32[7,18,1,128]{3,2,1,0:T(1,128)S(1)} collective-permute-done((f32[7,18,1,128]{3,2,1,0:T(1,128)S(1)}, f32[7,18,1,128]{3,2,1,0:T(1,128)S(1)}, u32[]{:S(2)}, u32[]{:S(2)}) %collective-permute-start.3) | collective-permute-done | bytes 64544 | tf_op jit(solution)/shard_map/ppermute | solution.py:15
  29.2 0.0 copy-done.5
  29.2 0.0 copy-done.7
  29.2 0.0 copy-start.9
  29.2 0.6 copy-done.9
  29.8 0.0 copy-done.3
  29.8 0.0 copy-done
  29.8 0.0 copy-done.1
  29.8 0.3 pad_maximum_fusion.1
  30.1 0.5 fusion.27
  30.6 1.6 copy.38
  32.2 3.5 %collective-permute-start.4 = (f32[7,18,18,1]{2,0,3,1:T(8,128)}, f32[7,18,18,1]{2,0,3,1:T(8,128)S(1)}, u32[]{:S(2)}, u32[]{:S(2)}) collective-permute-start(f32[7,18,18,1]{2,0,3,1:T(8,128)} %copy.38), channel_id=1, source_target_pairs={{0,1},{1,2},{2,3},{3,4},{4,5},{5,6},{6,7},{8,9},{9,10},{10,11},{11... | collective-permute-start | bytes 27224 | tf_op jit(solution)/shard_map/ppermute | solution.py:14
  35.7 1.0 copy.39
  36.7 1.5 collective-permute-start.5
  38.1 0.6 compare_and_fusion
  38.7 0.0 collective-permute-done.4
  38.7 0.9 copy.40
  39.6 2.4 collective-permute-done.5
  42.1 1.8 copy.41
  43.8 4.9 %pad_maximum_fusion = f32[7,18,18,130]{3,2,1,0:T(8,128)S(1)} fusion(f32[7,18,18,1]{3,2,1,0:T(8,128)S(1)} %copy.41, f32[7,18,1,128]{3,2,1,0:T(1,128)} %copy-done.9, f32[7,1,16,128]{3,2,1,0:T(8,128)} %copy-done.5, f32[1,16,16,128]{3,2,1,0:T(8,128)} %bitcast.24, f32[3,16,16,128]{3,2,1,0:T(8,128)} %param.7, f32[3,16,16,128]{3,2,1,0:T(8,128)S(1)} %copy-done, ...), kind=kLoop, calls=%fused_computation.1 | loop fusion | flops 2358720 | bytes 2358720 | tf_op jit(solution)/shard_map/concatenate | solution.py:16
  48.8 0.0 copy-start.4
  48.8 0.2 slice_bitcast_fusion.2
  48.9 0.7 copy-done.4
  49.7 0.0 copy-start.2
  49.7 0.0 copy-start.6
  49.7 0.3 fusion.23
  50.0 0.2 fusion.29
  50.2 0.5 copy-done.2
  50.7 0.0 copy-done.6
  50.7 0.0 copy-done.8
  50.7 0.0 copy-done.10
  50.7 1.5 add_add_fusion
  52.2 7.4 %copy.44 = bf16[3,16,16,128]{0,3,2,1:T(8,128)(2,1)} copy(f32[3,16,16,128]{3,2,1,0:T(8,128)} %add_add_fusion) | data formatting | bytes 589824 | tf_op jit(solution)/shard_map/add | solution.py:68
  59.6 7.3 %gather_fusion = bf16[1024,3]{1,0:T(8,128)(2,1)S(1)} fusion(bf16[3,32768]{0,1:T(8,128)(2,1)} %bitcast.21, s32[1024]{0:T(1024)S(1)} %fusion.25), kind=kCustom, calls=%fused_computation | custom fusion | bytes 16384 | tf_op jit(solution)/shard_map/jit(_take)/gather | solution.py:70
  66.9 0.0 copy-done.12
  66.9 0.2 fusion.17
  67.1 0.1 copy.45
  67.3 0.0 copy-done.13
  67.3 1.0 convolution_multiply_fusion
  68.3 0.0 all-reduce.2.cloned.1.call-update
  68.3 244.5 %all-reduce.2.cloned.1.call-done = f32[128,128]{0,1:T(8,128)} async-done(((f32[128,128]{0,1:T(8,128)}), f32[128,128]{0,1:T(8,128)}) %all-reduce.2.cloned.1.call-update) | async-done | bytes 65552 | tf_op jit(solution)/shard_map/psum | solution.py:74
  312.8 0.9 copy.47
  313.7 0.9 fusion.24
  314.6 11.7 %cholesky.18 = f32[128,128]{1,0:T(8,128)S(1)} custom-call(f32[128,128]{1,0:T(8,128)S(1)} %fusion.24), custom_call_target="Cholesky" | custom-call | tf_op jit(solution)/shard_map/jit(cholesky)/cholesky | solution.py:29
  326.3 0.6 compare_reduce_fusion
  327.0 0.7 select_bitcast_fusion
  327.6 0.7 copy.48
  (7 shorter events, 0.1 us)
Async XLA Ops:
  7.2 22.7 %copy-start.3 = (f32[16,16,128]{2,1,0:T(8,128)S(1)}, f32[16,16,128]{2,1,0:T(8,128)}, u32[]{:S(2)}) copy-start(f32[16,16,128]{2,1,0:T(8,128)} %param.6) | copy-start | bytes 393220
  7.2 22.7 %copy-start = (f32[3,16,16,128]{3,2,1,0:T(8,128)S(1)}, f32[3,16,16,128]{3,2,1,0:T(8,128)}, u32[]{:S(2)}) copy-start(f32[3,16,16,128]{3,2,1,0:T(8,128)} %param.5) | copy-start | bytes 1179652
  7.2 22.7 %copy-start.1 = (f32[3,16,16,128]{3,2,1,0:T(8,128)S(1)}, f32[3,16,16,128]{3,2,1,0:T(8,128)}, u32[]{:S(2)}) copy-start(f32[3,16,16,128]{3,2,1,0:T(8,128)} %param.7) | copy-start | bytes 1179652
  7.2 18.4 %copy-start.11 = (s32[1024]{0:T(1024)S(1)}, s32[1024]{0:T(1024)}, u32[]{:S(2)}) copy-start(s32[1024]{0:T(1024)} %param.9) | copy-start | bytes 12292
  7.2 305.6 %all-reduce.2.cloned.1.call-start = ((), (), s32[]{:S(2)}) async-start(), calls=%async_computation | async-start | bytes 131072 | tf_op jit(solution)/shard_map/psum | solution.py:74
  8.2 5.2 %collective-permute-start = (f32[7,1,16,128]{3,2,1,0:T(8,128)S(1)}, f32[7,1,16,128]{3,2,1,0:T(8,128)S(1)}, u32[]{:S(2)}, u32[]{:S(2)}) collective-permute-start(f32[7,1,16,128]{3,2,1,0:T(8,128)S(1)} %get-tuple-element.18), channel_id=1, source_target_pairs={{0,64},{64,128},{128,192},{1,65},{65,129},{129,193},{2,66},{66,130... | collective-permute-start | bytes 172040 | tf_op jit(solution)/shard_map/ppermute | solution.py:14
  12.1 4.9 %collective-permute-start.1 = (f32[7,1,16,128]{3,2,1,0:T(8,128)S(1)}, f32[7,1,16,128]{3,2,1,0:T(8,128)S(1)}, u32[]{:S(2)}, u32[]{:S(2)}) collective-permute-start(f32[7,1,16,128]{3,2,1,0:T(8,128)S(1)} %get-tuple-element.19), channel_id=1, source_target_pairs={{64,0},{128,64},{192,128},{65,1},{129,65},{193,129},{66,2},{130,66... | collective-permute-start | bytes 172040 | tf_op jit(solution)/shard_map/ppermute | solution.py:15
  17.0 12.2 %copy-start.5 = (f32[7,1,16,128]{3,2,1,0:T(8,128)}, f32[7,1,16,128]{3,2,1,0:T(8,128)S(1)}, u32[]{:S(2)}) copy-start(f32[7,1,16,128]{3,2,1,0:T(8,128)S(1)} %collective-permute-done.1) | copy-start | bytes 172036
  18.4 7.2 %collective-permute-start.2 = (f32[7,18,1,128]{3,2,1,0:T(1,128)S(1)}, f32[7,18,1,128]{3,2,1,0:T(1,128)S(1)}, u32[]{:S(2)}, u32[]{:S(2)}) collective-permute-start(f32[7,18,1,128]{3,2,1,0:T(1,128)S(1)} %get-tuple-element.16), channel_id=1, source_target_pairs={{0,8},{8,16},{16,24},{24,32},{32,40},{40,48},{48,56},{1,9},{9,17},... | collective-permute-start | bytes 193544 | tf_op jit(solution)/shard_map/ppermute | solution.py:14
  23.6 5.6 %collective-permute-start.3 = (f32[7,18,1,128]{3,2,1,0:T(1,128)S(1)}, f32[7,18,1,128]{3,2,1,0:T(1,128)S(1)}, u32[]{:S(2)}, u32[]{:S(2)}) collective-permute-start(f32[7,18,1,128]{3,2,1,0:T(1,128)S(1)} %get-tuple-element.17), channel_id=1, source_target_pairs={{8,0},{16,8},{24,16},{32,24},{40,32},{48,40},{56,48},{9,1},{17,9},... | collective-permute-start | bytes 193544 | tf_op jit(solution)/shard_map/ppermute | solution.py:15
  25.6 3.6 %copy-start.7 = (f32[7,18,1,128]{3,2,1,0:T(1,128)}, f32[7,18,1,128]{3,2,1,0:T(1,128)S(1)}, u32[]{:S(2)}) copy-start(f32[7,18,1,128]{3,2,1,0:T(1,128)S(1)} %collective-permute-done.2) | copy-start | bytes 193540
  29.2 0.6 copy-start.9
  32.2 6.5 %collective-permute-start.4 = (f32[7,18,18,1]{2,0,3,1:T(8,128)}, f32[7,18,18,1]{2,0,3,1:T(8,128)S(1)}, u32[]{:S(2)}, u32[]{:S(2)}) collective-permute-start(f32[7,18,18,1]{2,0,3,1:T(8,128)} %copy.38), channel_id=1, source_target_pairs={{0,1},{1,2},{2,3},{3,4},{4,5},{5,6},{6,7},{8,9},{9,10},{10,11},{11... | collective-permute-start | bytes 27224 | tf_op jit(solution)/shard_map/ppermute | solution.py:14
  36.7 5.4 %collective-permute-start.5 = (f32[7,18,18,1]{2,0,3,1:T(8,128)S(1)}, f32[7,18,18,1]{2,0,3,1:T(8,128)}, u32[]{:S(2)}, u32[]{:S(2)}) collective-permute-start(f32[7,18,18,1]{2,0,3,1:T(8,128)S(1)} %copy.39), channel_id=1, source_target_pairs={{1,0},{2,1},{3,2},{4,3},{5,4},{6,5},{7,6},{9,8},{10,9},{11,10},{12... | collective-permute-start | bytes 27224 | tf_op jit(solution)/shard_map/ppermute | solution.py:15
  48.8 0.9 copy-start.4
  49.7 1.0 copy-start.2
  49.7 1.0 copy-start.6
  49.7 1.0 copy-start.8
  49.7 1.0 copy-start.10
  52.2 14.8 %copy-start.12 = (pred[1024]{0:T(1024)(128)(4,1)S(1)}, pred[1024]{0:T(1024)(128)(4,1)}, u32[]{:S(2)}) copy-start(pred[1024]{0:T(1024)(128)(4,1)} %compare_and_fusion) | copy-start | bytes 3076
  52.2 15.1 %copy-start.13 = (bf16[127,3072]{1,0:T(8,128)(2,1)S(1)}, bf16[127,3072]{1,0:T(8,128)(2,1)}, u32[]{:S(2)}) copy-start(bf16[127,3072]{1,0:T(8,128)(2,1)} %param.8) | copy-start | bytes 2340868
Sparse Core Ops, SparseCore 0:
  68.5 244.2 all-reduce.1
where the time goes:
time: 336 us; the launch traced here: 335 us
  waiting for transfers between devices  254 us (76%)
  local copies, waits for them, and re-layouts  24.4 us (7%)
  other arithmetic  24 us (7%)
  starting transfers between devices  17.4 us (5%)
  between operations  14.3 us (4%)
    psum x1, waiting for transfers between devices, per_device(): whole_gram = lax.psum(local_gram, ('gx', 'gy', 'gz'))  244 us
    ppermute x3, starting transfers between devices, with_halo(): before = lax.ppermute(last, axis, up)  12.7 us
    another operation x3, other arithmetic, upper_factor(): return jnp.linalg.cholesky(gram).T  12.4 us
    ppermute x3, waiting for transfers between devices, with_halo(): after = lax.ppermute(first, axis, down)  9.65 us
    add x1, local copies, waits for them, and re-layouts, per_device(): new_fields = fields + (terms[0] + terms[1] + terms[2])  7.41 us
    gather x1, local copies, waits for them, and re-layouts, per_device(): sampled = jnp.take(flat_cells, sample_index, axis=1)  7.33 us
  transfers between devices with their start and end apart: 7, of which 4 were waited for; matrix products, arithmetic and copies ran while one was open for 1% of the time, Pallas kernels for 0%

commit v1 on v0

v1 whole, which is shorter than its diff:
```python
import functools

import jax
import jax.numpy as jnp
from jax import lax
from jax.experimental import pallas as pl
from jax.experimental.pallas import tpu as pltpu
from jax.sharding import PartitionSpec as P

MESH = pl.DeviceIdType.MESH
SNAPS = 128
STRIDE = 32


def lanes(shape):
    return lax.broadcasted_iota(jnp.int32, shape, len(shape) - 1)


def rows(shape):
    return lax.broadcasted_iota(jnp.int32, shape, len(shape) - 2)


def step_kernel(
    sizes,
    u_hbm, k_hbm, v_hbm, s_hbm, idx_ref,
    new_hbm, gram_ref,
    u_pad, k_pad, vx_pad, vyz, snaps, new_vmem, hy_u, hy_v, hy_k, hz_send, hz, pick, chosen, column,
    pieces, parts, zparts, full, col_parts, col_zparts,
    load_sem, store_sem, halo_send, halo_recv, mat_send, mat_recv, zmat_send, zmat_recv,
    all_send, all_recv, col_send, col_recv, zcol_send, zcol_recv,
):
    nx, ny, nz = sizes
    plane = nx * ny
    cx, cy, cz = k_hbm.shape
    x, y, z = lax.axis_index("gx"), lax.axis_index("gy"), lax.axis_index("gz")
    me = x * ny + y

    loads = [
        pltpu.make_async_copy(s_hbm, snaps, load_sem.at[0]),
        pltpu.make_async_copy(u_hbm, u_pad.at[:, pl.ds(1, cx)], load_sem.at[1]),
        pltpu.make_async_copy(k_hbm, k_pad.at[pl.ds(1, cx)], load_sem.at[2]),
        pltpu.make_async_copy(v_hbm.at[0], vx_pad.at[pl.ds(1, cx)], load_sem.at[3]),
        pltpu.make_async_copy(v_hbm.at[pl.ds(1, 2)], vyz, load_sem.at[4]),
    ]
    for load in loads:
        load.start()

    def plane_peer(j):
        peer = lax.rem(me + j, plane)
        return peer, (lax.div(peer, ny), lax.rem(peer, ny), z)

    def line_peer(j):
        return (x, y, lax.rem(z + j, nz))

    barrier = pltpu.get_barrier_semaphore()

    def greet_plane(j, carry):
        pl.semaphore_signal(barrier, inc=1, device_id=plane_peer(j)[1], device_id_type=MESH)
        return carry

    def greet_line(j, carry):
        pl.semaphore_signal(barrier, inc=1, device_id=line_peer(j), device_id_type=MESH)
        return carry

    lax.fori_loop(1, plane, greet_plane, 0)
    lax.fori_loop(1, nz, greet_line, 0)

    loads[0].wait()
    block = snaps[...]
    gram = lax.dot_general(
        block, block, (((1,), (1,)), ((), ())), preferred_element_type=jnp.float32
    )
    gram_ref[...] = jnp.zeros_like(gram_ref)
    gram_ref[0:SNAPS - 1, 0:SNAPS - 1] = gram
    per = SNAPS // plane
    for i in range(plane):
        pieces[i] = gram_ref[i * per:(i + 1) * per]

    for load in loads[1:]:
        load.wait()
    lane = lanes((cy, cz))

    def pack_layer(i, faces):
        low, high = faces
        arrays = [u_pad[0, i + 1], u_pad[1, i + 1], u_pad[2, i + 1], vyz[1, i], k_pad[i + 1]]
        for a, values in enumerate(arrays):
            spot = a * cx + i
            low = jnp.where(lane == spot, pltpu.roll(values, spot, 1), low)
            high = jnp.where(lane == spot, pltpu.roll(values, spot + 1, 1), high)
        return low, high

    empty = jnp.zeros((cy, cz), jnp.float32)
    low, high = lax.fori_loop(0, cx, pack_layer, (empty, empty))
    hz_send[0] = low
    hz_send[1] = high

    pl.semaphore_wait(barrier, plane - 1 + nz - 1)

    def send(src, dst, side, number, device):
        return pltpu.make_async_remote_copy(
            src_ref=src, dst_ref=dst, send_sem=halo_send.at[side, number],
            recv_sem=halo_recv.at[side, number], device_id=device, device_id_type=MESH,
        )

    up_x, down_x = lax.rem(x + 1, nx), lax.rem(x + nx - 1, nx)
    up_y, down_y = lax.rem(y + 1, ny), lax.rem(y + ny - 1, ny)
    up_z, down_z = lax.rem(z + 1, nz), lax.rem(z + nz - 1, nz)
    halos = [
        send(hz_send.at[1], hz.at[0], 4, 0, (x, y, up_z)),
        send(hz_send.at[0], hz.at[1], 5, 0, (x, y, down_z)),
        send(u_hbm.at[:, cx - 1], u_pad.at[:, 0], 0, 0, (up_x, y, z)),
        send(v_hbm.at[0, cx - 1], vx_pad.at[0], 0, 1, (up_x, y, z)),
        send(k_hbm.at[cx - 1], k_pad.at[0], 0, 2, (up_x, y, z)),
        send(u_hbm.at[:, 0], u_pad.at[:, cx + 1], 1, 0, (down_x, y, z)),
        send(v_hbm.at[0, 0], vx_pad.at[cx + 1], 1, 1, (down_x, y, z)),
        send(k_hbm.at[0], k_pad.at[cx + 1], 1, 2, (down_x, y, z)),
        send(u_hbm.at[:, :, cy - 1], hy_u.at[0], 2, 0, (x, up_y, z)),
        send(v_hbm.at[1, :, cy - 1], hy_v.at[0], 2, 1, (x, up_y, z)),
        send(k_hbm.at[:, cy - 1], hy_k.at[0], 2, 2, (x, up_y, z)),
        send(u_hbm.at[:, :, 0], hy_u.at[1], 3, 0, (x, down_y, z)),
        send(v_hbm.at[1, :, 0], hy_v.at[1], 3, 1, (x, down_y, z)),
        send(k_hbm.at[:, 0], hy_k.at[1], 3, 2, (x, down_y, z)),
    ]
    for halo in halos:
        halo.start()

    def send_piece(j, carry):
        peer, device = plane_peer(j)
        pltpu.make_async_remote_copy(
            src_ref=pieces.at[peer], dst_ref=parts.at[me], send_sem=mat_send, recv_sem=mat_recv,
            device_id=device, device_id_type=MESH,
        ).start()
        return carry

    lax.fori_loop(1, plane, send_piece, 0)
    parts[me] = pieces[me]

    wide = lanes((cx * cy, cz))
    offset = (idx_ref[...] & (STRIDE - 1)).astype(jnp.float32)
    samples = cz // STRIDE
    group = cz // samples
    spread = jnp.broadcast_to(offset[:, None, :], (cx * cy // group, group, cz)).reshape(cx * cy, cz)
    own = lax.div(wide, samples) == lax.rem(rows((cx * cy, cz)), group)
    spread = jnp.where(own, spread, 0.0).astype(jnp.bfloat16)
    square = (cz, cz)
    to_cells = (lax.rem(rows(square), samples) == lax.div(lanes(square), STRIDE)).astype(jnp.bfloat16)
    at = jnp.dot(spread, to_cells, preferred_element_type=jnp.float32)
    hit = at.astype(jnp.int32) == lax.rem(wide, STRIDE)
    pick[...] = jnp.where(hit, 1.0, 0.0).reshape(cx, cy, cz)

    for halo in halos:
        halo.wait_recv()

    @pl.when(x == 0)
    def _():
        u_pad[:, 0] = jnp.zeros_like(u_pad[:, 0])
        vx_pad[0] = jnp.zeros_like(vx_pad[0])
        k_pad[0] = jnp.zeros_like(k_pad[0])

    @pl.when(x == nx - 1)
    def _():
        u_pad[:, cx + 1] = jnp.zeros_like(u_pad[:, cx + 1])
        vx_pad[cx + 1] = jnp.zeros_like(vx_pad[cx + 1])
        k_pad[cx + 1] = jnp.zeros_like(k_pad[cx + 1])

    @pl.when(y == 0)
    def _():
        hy_u[0] = jnp.zeros_like(hy_u[0])
        hy_v[0] = jnp.zeros_like(hy_v[0])
        hy_k[0] = jnp.zeros_like(hy_k[0])

    @pl.when(y == ny - 1)
    def _():
        hy_u[1] = jnp.zeros_like(hy_u[1])
        hy_v[1] = jnp.zeros_like(hy_v[1])
        hy_k[1] = jnp.zeros_like(hy_k[1])

    @pl.when(z == 0)
    def _():
        hz[0] = jnp.zeros_like(hz[0])

    @pl.when(z == nz - 1)
    def _():
        hz[1] = jnp.zeros_like(hz[1])

    row = rows((cy, cz))

    def step_layer(i, carry):
        z_low, z_high = hz[0], hz[1]

        def y_sides(values, below, above):
            plus = jnp.where(row == cy - 1, above, pltpu.roll(values, cy - 1, 0))
            minus = jnp.where(row == 0, below, pltpu.roll(values, 1, 0))
            return plus, minus

        def z_sides(values, a):
            spot = a * cx + i
            plus = jnp.where(
                lane == cz - 1, pltpu.roll(z_high, cz - 1 - spot, 1), pltpu.roll(values, cz - 1, 1)
            )
            minus = jnp.where(lane == 0, pltpu.roll(z_low, cz - spot, 1), pltpu.roll(values, 1, 1))
            return plus, minus

        center_k = k_pad[i + 1]
        k_sides = [
            (k_pad[i + 2], k_pad[i]),
            y_sides(center_k, hy_k[0, pl.ds(i, 1)], hy_k[1, pl.ds(i, 1)]),
            z_sides(center_k, 4),
        ]
        v_sides = [
            (vx_pad[i + 2], vx_pad[i]),
            y_sides(vyz[0, i], hy_v[0, pl.ds(i, 1)], hy_v[1, pl.ds(i, 1)]),
            z_sides(vyz[1, i], 3),
        ]
        faces = [(0.5 * (plus + center_k), 0.5 * (center_k + minus)) for plus, minus in k_sides]
        speeds = [(0.5 * plus, 0.5 * minus) for plus, minus in v_sides]
        marked = pick[i] > 0.5
        for f in range(3):
            center = u_pad[f, i + 1]
            u_sides = [
                (u_pad[f, i + 2], u_pad[f, i]),
                y_sides(center, hy_u[0, f, pl.ds(i, 1)], hy_u[1, f, pl.ds(i, 1)]),
                z_sides(center, f),
            ]
            terms = []
            for (k_up, k_down), (v_up, v_down), (plus, minus) in zip(faces, speeds, u_sides):
                terms.append(
                    k_up * (plus - center) - k_down * (center - minus) - (v_up * plus - v_down * minus)
                )
            fresh = center + (terms[0] + terms[1] + terms[2])
            new_vmem[f, i] = fresh
            chosen[f, i] = jnp.where(marked, fresh, 0.0).astype(jnp.bfloat16)
        return carry

    lax.fori_loop(0, cx, step_layer, 0)
    store = pltpu.make_async_copy(new_vmem, new_hbm, store_sem)
    store.start()

    spots = 3 * cx * cy
    by_row = jnp.dot(
        chosen[...].reshape(spots, cz),
        (lax.div(rows(square), STRIDE) == lax.rem(lanes(square), samples)).astype(jnp.bfloat16),
        preferred_element_type=jnp.float32,
    ).reshape(spots // group, group, cz)
    own = lax.div(lanes((1, group, cz)), samples) == rows((1, group, cz))
    fresh_rows = jnp.sum(jnp.where(own, by_row, 0.0), axis=1)
    column[...] = jnp.zeros_like(column)
    for i in range(spots // group):
        column[0:1, i * cz:(i + 1) * cz] = fresh_rows[i:i + 1]
    line = lax.dot_general(
        column[...].astype(jnp.bfloat16), snaps[...], (((1,), (1,)), ((), ())),
        preferred_element_type=jnp.float32,
    )
    own_square = jnp.sum(jnp.sum(fresh_rows * fresh_rows, axis=0, keepdims=True), axis=1, keepdims=True)
    last = lanes((1, SNAPS)) == SNAPS - 1
    column[:, 0:SNAPS - 1] = line
    col_parts[me] = jnp.where(last, own_square, column[0:1, 0:SNAPS])

    def send_column(j, carry):
        peer, device = plane_peer(j)
        pltpu.make_async_remote_copy(
            src_ref=col_parts.at[me], dst_ref=col_parts.at[me], send_sem=col_send, recv_sem=col_recv,
            device_id=device, device_id_type=MESH,
        ).start()
        return carry

    lax.fori_loop(1, plane, send_column, 0)

    def arrived(ref, sem, count):
        pltpu.make_async_copy(ref.at[pl.ds(0, count)], ref.at[pl.ds(0, count)], sem).wait()

    arrived(parts, mat_recv, plane - 1)
    zparts[z] = jnp.sum(parts[...], axis=0)

    def send_sum(j, carry):
        pltpu.make_async_remote_copy(
            src_ref=zparts.at[z], dst_ref=zparts.at[z], send_sem=zmat_send, recv_sem=zmat_recv,
            device_id=line_peer(j), device_id_type=MESH,
        ).start()
        return carry

    lax.fori_loop(1, nz, send_sum, 0)

    arrived(col_parts, col_recv, plane - 1)
    col_zparts[z] = jnp.sum(col_parts[...], axis=0)

    def send_column_sum(j, carry):
        pltpu.make_async_remote_copy(
            src_ref=col_zparts.at[z], dst_ref=col_zparts.at[z], send_sem=zcol_send, recv_sem=zcol_recv,
            device_id=line_peer(j), device_id_type=MESH,
        ).start()
        return carry

    lax.fori_loop(1, nz, send_column_sum, 0)

    arrived(zparts, zmat_recv, nz - 1)
    full[me] = jnp.sum(zparts[...], axis=0)

    def send_total(j, carry):
        peer, device = plane_peer(j)
        pltpu.make_async_remote_copy(
            src_ref=full.at[me], dst_ref=full.at[me], send_sem=all_send, recv_sem=all_recv,
            device_id=device, device_id_type=MESH,
        ).start()
        return carry

    lax.fori_loop(1, plane, send_total, 0)

    arrived(col_zparts, zcol_recv, nz - 1)
    total_column = jnp.sum(col_zparts[...], axis=0)
    arrived(full, all_recv, plane - 1)

    scale = 1.0 / (SNAPS // SNAPS * s_hbm.shape[1] * plane * nz)
    for i in range(plane):
        gram_ref[i * per:(i + 1) * per] = full[i] * scale
    gram_ref[SNAPS - 1:SNAPS] = total_column * scale

    store.wait()
    for halo in halos:
        halo.wait_send()
    arrived(pieces, mat_send, plane - 1)
    arrived(zparts, zmat_send, nz - 1)
    arrived(full, all_send, plane - 1)
    arrived(col_parts, col_send, plane - 1)
    arrived(col_zparts, zcol_send, nz - 1)


def per_device(sizes, fields, diffusivity, velocity, stored_snapshots, sample_index):
    nx, ny, nz = sizes
    plane = nx * ny
    _, cx, cy, cz = fields.shape
    per = SNAPS // plane
    f32, dma = jnp.float32, pltpu.SemaphoreType.DMA
    anywhere = pl.BlockSpec(memory_space=pl.ANY)
    vmem = pl.BlockSpec(memory_space=pltpu.VMEM)
    index = sample_index.reshape(-1, cz)
    new_fields, gram = pl.pallas_call(
        functools.partial(step_kernel, sizes),
        out_shape=(
            jax.ShapeDtypeStruct(fields.shape, f32),
            jax.ShapeDtypeStruct((SNAPS, SNAPS), f32),
        ),
        in_specs=[anywhere] * 4 + [vmem],
        out_specs=(anywhere, vmem),
        scratch_shapes=[
            pltpu.VMEM((3, cx + 2, cy, cz), f32),
            pltpu.VMEM((cx + 2, cy, cz), f32),
            pltpu.VMEM((cx + 2, cy, cz), f32),
            pltpu.VMEM((2, cx, cy, cz), f32),
            pltpu.VMEM(stored_snapshots.shape, jnp.bfloat16),
            pltpu.VMEM((3, cx, cy, cz), f32),
            pltpu.VMEM((2, 3, cx, cz), f32),
            pltpu.VMEM((2, cx, cz), f32),
            pltpu.VMEM((2, cx, cz), f32),
            pltpu.VMEM((2, cy, cz), f32),
            pltpu.VMEM((2, cy, cz), f32),
            pltpu.VMEM((cx, cy, cz), f32),
            pltpu.VMEM((3, cx, cy, cz), jnp.bfloat16),
            pltpu.VMEM((8, stored_snapshots.shape[1]), f32),
            pltpu.VMEM((plane, per, SNAPS), f32),
            pltpu.VMEM((plane, per, SNAPS), f32),
            pltpu.VMEM((nz, per, SNAPS), f32),
            pltpu.VMEM((plane, per, SNAPS), f32),
            pltpu.VMEM((plane, 1, SNAPS), f32),
            pltpu.VMEM((nz, 1, SNAPS), f32),
            dma((5,)),
            dma,
            dma((6, 3)),
            dma((6, 3)),
        ] + [dma] * 10,
        compiler_params=pltpu.CompilerParams(collective_id=0, has_side_effects=True),
        name="step",
    )(fields, diffusivity, velocity, stored_snapshots, index)
    snapshot_r = lax.linalg.cholesky(gram, symmetrize_input=False).T
    return (new_fields, snapshot_r)


def solution(mesh):
    sizes = tuple(mesh.shape[axis] for axis in ("gx", "gy", "gz"))
    placed = (
        P(None, "gx", "gy", "gz"),
        P("gx", "gy", "gz"),
        P(None, "gx", "gy", "gz"),
        P(None, ("gx", "gy", "gz")),
        P(("gx", "gy", "gz")),
    )
    return jax.shard_map(
        functools.partial(per_device, sizes),
        mesh=mesh,
        in_specs=placed,
        out_specs=(P(None, "gx", "gy", "gz"), P()),
        check_vma=False,
    )
```

time: 336 us -> 46.3 us (0.14)
  waiting for transfers between devices: 254 us -> 0 us
  Pallas kernels: 0 us -> 29 us
  local copies, waits for them, and re-layouts: 24.4 us -> 2.5 us
  starting transfers between devices: 17.4 us -> 0 us
  between operations: 14.3 us -> 0.66 us
  other arithmetic: 24 us -> 13.9 us
    psum x1 -> x0, waiting for transfers between devices: 244 us -> none  [per_device(): whole_gram = lax.psum(local_gram, ('gx', 'gy', 'gz'))]
    pallas_call x0 -> x1, Pallas kernels: none -> 29 us  [per_device(): pl.pallas_call(functools.partial(step_kernel, sizes), out_shape=(jax.Shap...]
    ppermute x6 -> x0, starting transfers between devices: 17.3 us -> none  [the longest x3 12.7 us: with_halo(): before = lax.ppermute(last, axis, up)]
    ppermute x6 -> x0, waiting for transfers between devices: 9.66 us -> none  [the longest x3 9.65 us: with_halo(): after = lax.ppermute(first, axis, down)]
    add x1 -> x0, local copies, waits for them, and re-layouts: 7.41 us -> none  [per_device(): new_fields = fields + (terms[0] + terms[1] + terms[2])]
    gather x1 -> x0, local copies, waits for them, and re-layouts: 7.33 us -> none  [per_device(): sampled = jnp.take(flat_cells, sample_index, axis=1)]
    concatenate x2 -> x0, other arithmetic: 5.21 us -> none  [with_halo(): array = jnp.concatenate([before, array, after], axis=dim)]
  transfers between devices with their start and end apart: 7 -> 0, of which waited for: 4 -> 0; matrix products, arithmetic and copies ran while one was open for 1% -> 0% of each run, Pallas kernels for 0% -> 0%
where the time goes in v1:
time: 46.3 us; the launch traced here: 46 us
  Pallas kernels  29 us (63%)
  other arithmetic  13.9 us (30%)
  local copies, waits for them, and re-layouts  2.5 us (5%)
  between operations  0.66 us (1%)
    pallas_call x1, Pallas kernels, per_device(): pl.pallas_call(functools.partial(step_kernel, sizes), out_shape=(jax.Shap...  29 us
    another operation x3, other arithmetic, per_device(): snapshot_r = lax.linalg.cholesky(gram, symmetrize_input=False).T  13.2 us
    unnamed x2, local copies, waits for them, and re-layouts  2.5 us

profile of v1, /device:TPU:1, one launch (start us, length us, event | category | flops | bytes accessed | tf_op | source)
XLA Modules:
  0.0 46.0 jit_solution(8807894019656187284)
XLA Ops:
  0.6 29.0 %step.1 = (f32[3,16,16,128]{3,2,1,0:T(8,128)}, f32[128,128]{1,0:T(8,128)}) custom-call(f32[3,16,16,128]{3,2,1,0:T(8,128)} %u_hbm.1, f32[16,16,128]{2,1,0:T(8,128)} %k_hbm.1, f32[3,16,16,128]{3,2,1,0:T(8,128)} %v_hbm.1, bf16[127,3072]{1,0:T(8,128)(2,1)} %s_hbm.1, s32[8,128]{1,0:T(8,128)} %bitcast.3), custom_call_target="tpu_custom_call" | custom-call | tf_op jit(solution)/shard_map/step/pallas_call | solution.py:337
  29.6 12.5 %cholesky.18 = f32[128,128]{1,0:T(8,128)S(1)} custom-call(f32[128,128]{1,0:T(8,128)} %get-tuple-element.5), custom_call_target="Cholesky" | custom-call | tf_op jit(solution)/shard_map/cholesky | solution.py:374
  42.2 0.6 %compare_reduce_fusion = pred[]{:T(512)} fusion(f32[128]{0:T(128)S(1)} %select_reduce_fusion), kind=kLoop, calls=%fused_computation.4 | loop fusion | flops 255 | bytes 513 | tf_op jit(solution)/shard_map/cholesky | solution.py:374
  42.9 0.7 %select_bitcast_fusion = f32[128,128]{0,1:T(8,128)S(1)} fusion(f32[128,128]{1,0:T(8,128)S(1)} %cholesky.18, pred[]{:T(512)} %compare_reduce_fusion), kind=kLoop, calls=%fused_computation | loop fusion | flops 49152 | bytes 131073 | tf_op jit(solution)/shard_map/transpose | solution.py:374
  43.5 0.7 %copy.7 = f32[128,128]{1,0:T(8,128)} copy(f32[128,128]{0,1:T(8,128)S(1)} %select_bitcast_fusion) | data formatting | bytes 131072
  44.3 1.8 %copy.9 = f32[3,16,16,128]{3,2,1,0:T(8,128)} copy(f32[3,16,16,128]{3,2,1,0:T(8,128)} %get-tuple-element.10) | data formatting | bytes 786432
  (1 shorter events, 0.0 us)

commit v2 on v1

--- a/solution.py
+++ b/solution.py
@@ -323,6 +323,74 @@
     arrived(full, all_send, plane - 1)
     arrived(col_parts, col_send, plane - 1)
     arrived(col_zparts, zcol_send, nz - 1)
+
+
+def factor_kernel(gram_ref, new_in, r_ref, new_out, held, sem_in, sem_out):
+    size, edge = gram_ref.shape[0], 8
+    blocks = size // edge
+    tile = (edge, size)
+    fetch = pltpu.make_async_copy(new_in, held, sem_in)
+    keep = pltpu.make_async_copy(held, new_out, sem_out)
+    fetch.start()
+
+    last_lane = lanes(tile) == size - 1
+    turned = jnp.transpose(gram_ref[size - edge:size])
+    work = [
+        jnp.where(last_lane, turned[t * edge:(t + 1) * edge, edge - 1:edge], gram_ref[t * edge:(t + 1) * edge])
+        for t in range(blocks)
+    ]
+
+    def spread_lane(values, at):
+        return jnp.broadcast_to(values[:, at:at + 1], tile)
+
+    for b in range(blocks):
+        if b == 2:
+            fetch.wait()
+            keep.start()
+        base = b * edge
+        line = [jnp.broadcast_to(work[b][i:i + 1], tile) for i in range(edge)]
+        entry = [
+            [spread_lane(line[i], base + j) if j >= i else None for j in range(edge)]
+            for i in range(edge)
+        ]
+        ahead = b + 1 < blocks
+        if ahead:
+            following = work[b + 1]
+            side = [spread_lane(following, base + i) for i in range(edge)]
+        ratio_lines = []
+        for i in range(edge):
+            inverse = pl.reciprocal(entry[i][i], approx=False)
+            ratio = [entry[i][j] * inverse if j > i else None for j in range(edge)]
+            ratio_line = line[i] * inverse
+            ratio_lines.append(ratio_line)
+            for j in range(i + 1, edge):
+                for k in range(j, edge):
+                    entry[j][k] = entry[j][k] - ratio[j] * entry[i][k]
+            for j in range(i + 1, edge):
+                line[j] = line[j] - ratio[j] * line[i]
+            if ahead:
+                following = following - side[i] * ratio_line
+                for j in range(i + 1, edge):
+                    side[j] = side[j] - ratio[j] * side[i]
+        sub = rows(tile)
+        panel, ratios = line[0], ratio_lines[0]
+        root = lax.rsqrt(entry[0][0])
+        for i in range(1, edge):
+            panel = jnp.where(sub == i, line[i], panel)
+            ratios = jnp.where(sub == i, ratio_lines[i], ratios)
+            root = jnp.where(sub == i, lax.rsqrt(entry[i][i]), root)
+        r_ref[base:base + edge] = jnp.where(lanes(tile) >= sub + base, panel * root, 0.0)
+        if ahead:
+            work[b + 1] = following
+        if b + 2 < blocks:
+            flipped = jnp.transpose(ratios)
+            for t in range(b + 2, blocks):
+                chunk = flipped[t * edge:(t + 1) * edge]
+                value = work[t]
+                for i in range(edge):
+                    value = value - jnp.broadcast_to(chunk[:, i:i + 1], tile) * line[i]
+                work[t] = value
+    keep.wait()
 
 
 def per_device(sizes, fields, diffusivity, velocity, stored_snapshots, sample_index):
@@ -371,7 +439,17 @@
         compiler_params=pltpu.CompilerParams(collective_id=0, has_side_effects=True),
         name="step",
     )(fields, diffusivity, velocity, stored_snapshots, index)
-    snapshot_r = lax.linalg.cholesky(gram, symmetrize_input=False).T
+    snapshot_r, new_fields = pl.pallas_call(
+        factor_kernel,
+        out_shape=(
+            jax.ShapeDtypeStruct((SNAPS, SNAPS), f32),
+            jax.ShapeDtypeStruct(fields.shape, f32),
+        ),
+        in_specs=[vmem, anywhere],
+        out_specs=(vmem, anywhere),
+        scratch_shapes=[pltpu.VMEM(fields.shape, f32), dma, dma],
+        name="factor",
+    )(gram, new_fields)
     return (new_fields, snapshot_r)
 
 

time: 46.3 us -> 37.2 us (0.80)
  other arithmetic: 13.9 us -> 0 us
  Pallas kernels: 29 us -> 36.3 us
  local copies, waits for them, and re-layouts: 2.5 us -> 0 us
    another operation x3 -> x0, other arithmetic: 13.2 us -> none  [per_device(): snapshot_r = lax.linalg.cholesky(gram, symmetrize_input=False).T]
    pallas_call x0 -> x1, Pallas kernels: none -> 7.32 us  [per_device(): pl.pallas_call(factor_kernel, out_shape=(jax.ShapeDtypeStruct((SNAPS, SNA...]
    unnamed x2 -> x0, local copies, waits for them, and re-layouts: 2.5 us -> none
    transpose x1 -> x0, other arithmetic: 0.66 us -> none  [per_device(): snapshot_r = lax.linalg.cholesky(gram, symmetrize_input=False).T]
where the time goes in v2:
time: 37.2 us; the launch traced here: 37 us
  Pallas kernels  36.3 us (98%)
  between operations  0.64 us (2%)
    pallas_call x1, Pallas kernels, per_device(): pl.pallas_call(functools.partial(step_kernel, sizes), out_shape=(jax.Shap...  29 us
    pallas_call x1, Pallas kernels, per_device(): pl.pallas_call(factor_kernel, out_shape=(jax.ShapeDtypeStruct((SNAPS, SNA...  7.32 us

profile of v2, /device:TPU:1, one launch (start us, length us, event | category | flops | bytes accessed | tf_op | source)
XLA Modules:
  0.0 37.0 jit_solution(2197767267126102220)
XLA Ops:
  0.6 29.0 %step.1 = (f32[3,16,16,128]{3,2,1,0:T(8,128)}, f32[128,128]{1,0:T(8,128)}) custom-call(f32[3,16,16,128]{3,2,1,0:T(8,128)} %u_hbm.1, f32[16,16,128]{2,1,0:T(8,128)} %k_hbm.1, f32[3,16,16,128]{3,2,1,0:T(8,128)} %v_hbm.1, bf16[127,3072]{1,0:T(8,128)(2,1)} %s_hbm.1, s32[8,128]{1,0:T(8,128)} %bitcast.1), custom_call_target="tpu_custom_call" | custom-call | tf_op jit(solution)/shard_map/step/pallas_call | solution.py:405
  29.6 7.3 %factor.1 = (f32[128,128]{1,0:T(8,128)}, f32[3,16,16,128]{3,2,1,0:T(8,128)}) custom-call(f32[128,128]{1,0:T(8,128)} %get-tuple-element.6.gram_ref, f32[3,16,16,128]{3,2,1,0:T(8,128)} %get-tuple-element.7.new_in), custom_call_target="tpu_custom_call" | custom-call | tf_op jit(solution)/shard_map/factor/pallas_call | solution.py:442

commit v3 on v2

--- a/solution.py
+++ b/solution.py
@@ -9,6 +9,7 @@
 
 MESH = pl.DeviceIdType.MESH
 SNAPS = 128
+UNROLL = 4
 STRIDE = 32
 
 
@@ -22,9 +23,9 @@
 
 def step_kernel(
     sizes,
-    u_hbm, k_hbm, v_hbm, s_hbm, idx_ref,
+    u_hbm, k_hbm, v_hbm, s_hbm, idx_hbm,
     new_hbm, gram_ref,
-    u_pad, k_pad, vx_pad, vyz, snaps, new_vmem, hy_u, hy_v, hy_k, hz_send, hz, pick, chosen, column,
+    idx_ref, u_pad, k_pad, vx_pad, vyz, snaps, new_vmem, hy_u, hy_v, hy_k, hz_send, hz, pick, chosen, column,
     pieces, parts, zparts, full, col_parts, col_zparts,
     load_sem, store_sem, halo_send, halo_recv, mat_send, mat_recv, zmat_send, zmat_recv,
     all_send, all_recv, col_send, col_recv, zcol_send, zcol_recv,
@@ -41,29 +42,38 @@
         pltpu.make_async_copy(k_hbm, k_pad.at[pl.ds(1, cx)], load_sem.at[2]),
         pltpu.make_async_copy(v_hbm.at[0], vx_pad.at[pl.ds(1, cx)], load_sem.at[3]),
         pltpu.make_async_copy(v_hbm.at[pl.ds(1, 2)], vyz, load_sem.at[4]),
+        pltpu.make_async_copy(idx_hbm, idx_ref, load_sem.at[5]),
     ]
     for load in loads:
         load.start()
 
-    def plane_peer(j):
-        peer = lax.rem(me + j, plane)
-        return peer, (lax.div(peer, ny), lax.rem(peer, ny), z)
-
-    def line_peer(j):
-        return (x, y, lax.rem(z + j, nz))
+    near_x = [lax.rem(x + j, nx) for j in range(nx)]
+    near_y = [lax.rem(y + j, ny) for j in range(ny)]
+    plane_peers = [(px, py) for px in near_x for py in near_y][1:]
+    line_peers = [lax.rem(z + j, nz) for j in range(1, nz)]
 
     barrier = pltpu.get_barrier_semaphore()
-
-    def greet_plane(j, carry):
-        pl.semaphore_signal(barrier, inc=1, device_id=plane_peer(j)[1], device_id_type=MESH)
-        return carry
-
-    def greet_line(j, carry):
-        pl.semaphore_signal(barrier, inc=1, device_id=line_peer(j), device_id_type=MESH)
-        return carry
-
-    lax.fori_loop(1, plane, greet_plane, 0)
-    lax.fori_loop(1, nz, greet_line, 0)
+    for peer in plane_peers:
+        pl.semaphore_signal(barrier, inc=1, device_id=(*peer, z), device_id_type=MESH)
+    for peer in line_peers:
+        pl.semaphore_signal(barrier, inc=1, device_id=(x, y, peer), device_id_type=MESH)
+
+    def to_plane(src, dst, send_sem, recv_sem):
+        for peer in plane_peers:
+            pltpu.make_async_remote_copy(
+                src_ref=src(peer), dst_ref=dst, send_sem=send_sem, recv_sem=recv_sem,
+                device_id=(*peer, z), device_id_type=MESH,
+            ).start()
+
+    def to_line(ref, send_sem, recv_sem):
+        for peer in line_peers:
+            pltpu.make_async_remote_copy(
+                src_ref=ref.at[z], dst_ref=ref.at[z], send_sem=send_sem, recv_sem=recv_sem,
+                device_id=(x, y, peer), device_id_type=MESH,
+            ).start()
+
+    def arrived(ref, sem, count):
+        pltpu.make_async_copy(ref.at[pl.ds(0, count)], ref.at[pl.ds(0, count)], sem).wait()
 
     loads[0].wait()
     block = snaps[...]
@@ -80,26 +90,38 @@
         load.wait()
     lane = lanes((cy, cz))
 
-    def pack_layer(i, faces):
-        low, high = faces
+    low = high = jnp.zeros((cy, cz), jnp.float32)
+    for i in range(cx):
         arrays = [u_pad[0, i + 1], u_pad[1, i + 1], u_pad[2, i + 1], vyz[1, i], k_pad[i + 1]]
         for a, values in enumerate(arrays):
             spot = a * cx + i
-            low = jnp.where(lane == spot, pltpu.roll(values, spot, 1), low)
-            high = jnp.where(lane == spot, pltpu.roll(values, spot + 1, 1), high)
-        return low, high
-
-    empty = jnp.zeros((cy, cz), jnp.float32)
-    low, high = lax.fori_loop(0, cx, pack_layer, (empty, empty))
+            here = lane == spot
+            low = jnp.where(here, pltpu.roll(values, spot, 1) if spot else values, low)
+            high = jnp.where(here, pltpu.roll(values, spot + 1, 1), high)
     hz_send[0] = low
     hz_send[1] = high
 
+    wide = lanes((cx * cy, cz))
+    offset = (idx_ref[...] & (STRIDE - 1)).astype(jnp.float32)
+    samples = cz // STRIDE
+    group = cz // samples
+    spread = jnp.broadcast_to(offset[:, None, :], (cx * cy // group, group, cz)).reshape(cx * cy, cz)
+    own = lax.div(wide, samples) == lax.rem(rows((cx * cy, cz)), group)
+    spread = jnp.where(own, spread, 0.0).astype(jnp.bfloat16)
+    square = (cz, cz)
+    to_cells = (lax.rem(rows(square), samples) == lax.div(lanes(square), STRIDE)).astype(jnp.bfloat16)
+    at = jnp.dot(spread, to_cells, preferred_element_type=jnp.float32)
+    hit = at.astype(jnp.int32) == lax.rem(wide, STRIDE)
+    pick[...] = jnp.where(hit, 1.0, 0.0).reshape(cx, cy, cz)
     pl.semaphore_wait(barrier, plane - 1 + nz - 1)
 
-    def send(src, dst, side, number, device):
+    to_plane(lambda peer: pieces.at[peer[0] * ny + peer[1]], parts.at[me], mat_send, mat_recv)
+    parts[me] = pieces[me]
+
+    def send(src, dst, side, number, target):
         return pltpu.make_async_remote_copy(
             src_ref=src, dst_ref=dst, send_sem=halo_send.at[side, number],
-            recv_sem=halo_recv.at[side, number], device_id=device, device_id_type=MESH,
+            recv_sem=halo_recv.at[side, number], device_id=target, device_id_type=MESH,
         )
 
     up_x, down_x = lax.rem(x + 1, nx), lax.rem(x + nx - 1, nx)
@@ -124,30 +146,6 @@
     for halo in halos:
         halo.start()
 
-    def send_piece(j, carry):
-        peer, device = plane_peer(j)
-        pltpu.make_async_remote_copy(
-            src_ref=pieces.at[peer], dst_ref=parts.at[me], send_sem=mat_send, recv_sem=mat_recv,
-            device_id=device, device_id_type=MESH,
-        ).start()
-        return carry
-
-    lax.fori_loop(1, plane, send_piece, 0)
-    parts[me] = pieces[me]
-
-    wide = lanes((cx * cy, cz))
-    offset = (idx_ref[...] & (STRIDE - 1)).astype(jnp.float32)
-    samples = cz // STRIDE
-    group = cz // samples
-    spread = jnp.broadcast_to(offset[:, None, :], (cx * cy // group, group, cz)).reshape(cx * cy, cz)
-    own = lax.div(wide, samples) == lax.rem(rows((cx * cy, cz)), group)
-    spread = jnp.where(own, spread, 0.0).astype(jnp.bfloat16)
-    square = (cz, cz)
-    to_cells = (lax.rem(rows(square), samples) == lax.div(lanes(square), STRIDE)).astype(jnp.bfloat16)
-    at = jnp.dot(spread, to_cells, preferred_element_type=jnp.float32)
-    hit = at.astype(jnp.int32) == lax.rem(wide, STRIDE)
-    pick[...] = jnp.where(hit, 1.0, 0.0).reshape(cx, cy, cz)
-
     for halo in halos:
         halo.wait_recv()
 
@@ -185,7 +183,7 @@
 
     row = rows((cy, cz))
 
-    def step_layer(i, carry):
+    def step_layer(i):
         z_low, z_high = hz[0], hz[1]
 
         def y_sides(values, below, above):
@@ -230,11 +228,19 @@
             fresh = center + (terms[0] + terms[1] + terms[2])
             new_vmem[f, i] = fresh
             chosen[f, i] = jnp.where(marked, fresh, 0.0).astype(jnp.bfloat16)
+
+    def step_layers(group, carry):
+        for i in range(UNROLL):
+            step_layer(group * UNROLL + i)
         return carry
 
-    lax.fori_loop(0, cx, step_layer, 0)
+    lax.fori_loop(0, cx // UNROLL, step_layers, 0)
     store = pltpu.make_async_copy(new_vmem, new_hbm, store_sem)
     store.start()
+
+    arrived(parts, mat_recv, plane - 1)
+    zparts[z] = jnp.sum(parts[...], axis=0)
+    to_line(zparts, zmat_send, zmat_recv)
 
     spots = 3 * cx * cy
     by_row = jnp.dot(
@@ -256,64 +262,22 @@
     column[:, 0:SNAPS - 1] = line
     col_parts[me] = jnp.where(last, own_square, column[0:1, 0:SNAPS])
 
-    def send_column(j, carry):
-        peer, device = plane_peer(j)
-        pltpu.make_async_remote_copy(
-            src_ref=col_parts.at[me], dst_ref=col_parts.at[me], send_sem=col_send, recv_sem=col_recv,
-            device_id=device, device_id_type=MESH,
-        ).start()
-        return carry
-
-    lax.fori_loop(1, plane, send_column, 0)
-
-    def arrived(ref, sem, count):
-        pltpu.make_async_copy(ref.at[pl.ds(0, count)], ref.at[pl.ds(0, count)], sem).wait()
-
-    arrived(parts, mat_recv, plane - 1)
-    zparts[z] = jnp.sum(parts[...], axis=0)
-
-    def send_sum(j, carry):
-        pltpu.make_async_remote_copy(
-            src_ref=zparts.at[z], dst_ref=zparts.at[z], send_sem=zmat_send, recv_sem=zmat_recv,
-            device_id=line_peer(j), device_id_type=MESH,
-        ).start()
-        return carry
-
-    lax.fori_loop(1, nz, send_sum, 0)
+    to_plane(lambda peer: col_parts.at[me], col_parts.at[me], col_send, col_recv)
+
+    arrived(zparts, zmat_recv, nz - 1)
+    scale = 1.0 / (s_hbm.shape[1] * plane * nz)
+    full[me] = jnp.sum(zparts[...], axis=0) * scale
+    to_plane(lambda peer: full.at[me], full.at[me], all_send, all_recv)
 
     arrived(col_parts, col_recv, plane - 1)
     col_zparts[z] = jnp.sum(col_parts[...], axis=0)
-
-    def send_column_sum(j, carry):
-        pltpu.make_async_remote_copy(
-            src_ref=col_zparts.at[z], dst_ref=col_zparts.at[z], send_sem=zcol_send, recv_sem=zcol_recv,
-            device_id=line_peer(j), device_id_type=MESH,
-        ).start()
-        return carry
-
-    lax.fori_loop(1, nz, send_column_sum, 0)
-
-    arrived(zparts, zmat_recv, nz - 1)
-    full[me] = jnp.sum(zparts[...], axis=0)
-
-    def send_total(j, carry):
-        peer, device = plane_peer(j)
-        pltpu.make_async_remote_copy(
-            src_ref=full.at[me], dst_ref=full.at[me], send_sem=all_send, recv_sem=all_recv,
-            device_id=device, device_id_type=MESH,
-        ).start()
-        return carry
-
-    lax.fori_loop(1, plane, send_total, 0)
-
+    to_line(col_zparts, zcol_send, zcol_recv)
+
+    arrived(full, all_recv, plane - 1)
+    for i in range(plane):
+        gram_ref[i * per:(i + 1) * per] = full[i]
     arrived(col_zparts, zcol_recv, nz - 1)
-    total_column = jnp.sum(col_zparts[...], axis=0)
-    arrived(full, all_recv, plane - 1)
-
-    scale = 1.0 / (SNAPS // SNAPS * s_hbm.shape[1] * plane * nz)
-    for i in range(plane):
-        gram_ref[i * per:(i + 1) * per] = full[i] * scale
-    gram_ref[SNAPS - 1:SNAPS] = total_column * scale
+    gram_ref[SNAPS - 1:SNAPS] = jnp.sum(col_zparts[...], axis=0) * scale
 
     store.wait()
     for halo in halos:
@@ -333,63 +297,70 @@
     keep = pltpu.make_async_copy(held, new_out, sem_out)
     fetch.start()
 
+    def across(values, at):
+        return jnp.broadcast_to(values[:, at:at + 1], tile)
+
+    def down(values, at):
+        return jnp.broadcast_to(values[at:at + 1], tile)
+
     last_lane = lanes(tile) == size - 1
     turned = jnp.transpose(gram_ref[size - edge:size])
+    raw = [gram_ref[t * edge:(t + 1) * edge] for t in range(blocks)]
     work = [
-        jnp.where(last_lane, turned[t * edge:(t + 1) * edge, edge - 1:edge], gram_ref[t * edge:(t + 1) * edge])
+        jnp.where(last_lane, turned[t * edge:(t + 1) * edge, edge - 1:edge], raw[t])
         for t in range(blocks)
     ]
-
-    def spread_lane(values, at):
-        return jnp.broadcast_to(values[:, at:at + 1], tile)
+    sub = rows(tile)
 
     for b in range(blocks):
-        if b == 2:
+        if b == blocks // 2:
             fetch.wait()
             keep.start()
         base = b * edge
-        line = [jnp.broadcast_to(work[b][i:i + 1], tile) for i in range(edge)]
-        entry = [
-            [spread_lane(line[i], base + j) if j >= i else None for j in range(edge)]
-            for i in range(edge)
-        ]
         ahead = b + 1 < blocks
+        source = raw if b == 0 else work
+        column = [across(source[b], base + i) for i in range(edge)]
+        line = [down(work[b], i) for i in range(edge)]
         if ahead:
+            side = [across(source[b + 1], base + i) for i in range(edge)]
             following = work[b + 1]
-            side = [spread_lane(following, base + i) for i in range(edge)]
-        ratio_lines = []
+        panel = ratios = pivots = None
         for i in range(edge):
-            inverse = pl.reciprocal(entry[i][i], approx=False)
-            ratio = [entry[i][j] * inverse if j > i else None for j in range(edge)]
+            pivot = down(column[i], i)
+            inverse = pl.reciprocal(pivot, approx=False)
+            ratio = [down(column[j], i) * inverse if j > i else None for j in range(edge)]
             ratio_line = line[i] * inverse
-            ratio_lines.append(ratio_line)
             for j in range(i + 1, edge):
-                for k in range(j, edge):
-                    entry[j][k] = entry[j][k] - ratio[j] * entry[i][k]
+                column[j] = column[j] - ratio[j] * column[i]
             for j in range(i + 1, edge):
                 line[j] = line[j] - ratio[j] * line[i]
             if ahead:
                 following = following - side[i] * ratio_line
                 for j in range(i + 1, edge):
                     side[j] = side[j] - ratio[j] * side[i]
-        sub = rows(tile)
-        panel, ratios = line[0], ratio_lines[0]
-        root = lax.rsqrt(entry[0][0])
-        for i in range(1, edge):
-            panel = jnp.where(sub == i, line[i], panel)
-            ratios = jnp.where(sub == i, ratio_lines[i], ratios)
-            root = jnp.where(sub == i, lax.rsqrt(entry[i][i]), root)
-        r_ref[base:base + edge] = jnp.where(lanes(tile) >= sub + base, panel * root, 0.0)
+            panel = line[i] if i == 0 else jnp.where(sub == i, line[i], panel)
+            ratios = ratio_line if i == 0 else jnp.where(sub == i, ratio_line, ratios)
+            pivots = pivot if i == 0 else jnp.where(sub == i, pivot, pivots)
+        r_ref[base:base + edge] = jnp.where(
+            lanes(tile) >= sub + base, panel * lax.rsqrt(pivots), 0.0
+        )
         if ahead:
             work[b + 1] = following
         if b + 2 < blocks:
             flipped = jnp.transpose(ratios)
-            for t in range(b + 2, blocks):
-                chunk = flipped[t * edge:(t + 1) * edge]
-                value = work[t]
-                for i in range(edge):
-                    value = value - jnp.broadcast_to(chunk[:, i:i + 1], tile) * line[i]
-                work[t] = value
+            near = (b + 2) * edge
+            terms = [across(flipped[near:near + edge], i) * line[i] for i in range(edge)]
+            while len(terms) > 1:
+                terms = [p + q for p, q in zip(terms[::2], terms[1::2])]
+            work[b + 2] = work[b + 2] - terms[0]
+        if b + 3 < blocks:
+            far = (b + 3) * edge
+            update = jnp.dot(
+                flipped[far:], panel, precision=lax.Precision.HIGHEST,
+                preferred_element_type=jnp.float32,
+            )
+            for t in range(b + 3, blocks):
+                work[t] = work[t] - update[t * edge - far:(t + 1) * edge - far]
     keep.wait()
 
 
@@ -408,9 +379,10 @@
             jax.ShapeDtypeStruct(fields.shape, f32),
             jax.ShapeDtypeStruct((SNAPS, SNAPS), f32),
         ),
-        in_specs=[anywhere] * 4 + [vmem],
+        in_specs=[anywhere] * 5,
         out_specs=(anywhere, vmem),
         scratch_shapes=[
+            pltpu.VMEM(index.shape, jnp.int32),
             pltpu.VMEM((3, cx + 2, cy, cz), f32),
             pltpu.VMEM((cx + 2, cy, cz), f32),
             pltpu.VMEM((cx + 2, cy, cz), f32),
@@ -431,7 +403,7 @@
             pltpu.VMEM((plane, per, SNAPS), f32),
             pltpu.VMEM((plane, 1, SNAPS), f32),
             pltpu.VMEM((nz, 1, SNAPS), f32),
-            dma((5,)),
+            dma((6,)),
             dma,
             dma((6, 3)),
             dma((6, 3)),

time: 37.2 us -> 34 us (0.914)
  Pallas kernels: 36.3 us -> 33.2 us
    pallas_call x1, Pallas kernels: 29 us -> 26.9 us  [per_device(): pl.pallas_call(functools.partial(step_kernel, sizes), out_shape=(jax.Shap...]
    pallas_call x1, Pallas kernels: 7.32 us -> 6.29 us  [per_device(): pl.pallas_call(factor_kernel, out_shape=(jax.ShapeDtypeStruct((SNAPS, SNA...]
where the time goes in v3:
time: 34 us; the launch traced here: 33.8 us
  Pallas kernels  33.2 us (98%)
  between operations  0.64 us (2%)
    pallas_call x1, Pallas kernels, per_device(): pl.pallas_call(functools.partial(step_kernel, sizes), out_shape=(jax.Shap...  26.9 us
    pallas_call x1, Pallas kernels, per_device(): pl.pallas_call(factor_kernel, out_shape=(jax.ShapeDtypeStruct((SNAPS, SNA...  6.29 us

profile of v3, /device:TPU:1, one launch (start us, length us, event | category | flops | bytes accessed | tf_op | source)
XLA Modules:
  0.0 33.8 jit_solution(2193547787796965929)
XLA Ops:
  0.6 26.9 %step.1 = (f32[3,16,16,128]{3,2,1,0:T(8,128)}, f32[128,128]{1,0:T(8,128)}) custom-call(f32[3,16,16,128]{3,2,1,0:T(8,128)} %u_hbm.1, f32[16,16,128]{2,1,0:T(8,128)} %k_hbm.1, f32[3,16,16,128]{3,2,1,0:T(8,128)} %v_hbm.1, bf16[127,3072]{1,0:T(8,128)(2,1)} %s_hbm.1, s32[8,128]{1,0:T(8,128)} %bitcast.1), custom_call_target="tpu_custom_call" | custom-call | tf_op jit(solution)/shard_map/step/pallas_call | solution.py:376
  27.6 6.3 %factor.1 = (f32[128,128]{1,0:T(8,128)}, f32[3,16,16,128]{3,2,1,0:T(8,128)}) custom-call(f32[128,128]{1,0:T(8,128)} %get-tuple-element.6.gram_ref, f32[3,16,16,128]{3,2,1,0:T(8,128)} %get-tuple-element.7.new_in), custom_call_target="tpu_custom_call" | custom-call | tf_op jit(solution)/shard_map/factor/pallas_call | solution.py:414
